TPU v7x, 256 devices: a whole 4x4x8 slice. The times are simulated.
256 devices in a mesh: dp: 16 (over x, y_hi, core), ctx: 16 (over z, y_lo).
Axes of the slice: x: 4, y: 4 (y_hi: 2, y_lo: 2; y = y_hi * 2 + y_lo), z: 8, core: 2. Of those that a mesh axis runs over, the one named last changes fastest.
Arguments:
- query_frames: bfloat16 [65536, 2560], P(('dp', 'ctx')), parts along dimension 0, may hold values from -8 to 8
- key_frames: bfloat16 [65536, 2560], P(('dp', 'ctx')), parts along dimension 0, may hold values from -8 to 8
- value_frames: bfloat16 [65536, 2560], P(('dp', 'ctx')), parts along dimension 0, may hold values from -6 to 6
- stream: bfloat16 [65536, 5120], P(('dp', 'ctx')), parts along dimension 0, may hold values from -1.25 to 1.25
- out_weight: bfloat16 [2560, 5120], P('ctx'), may hold values from -0.125 to 0.125
Outputs:
- layer_out: bfloat16 [65536, 5120], P(('dp', 'ctx')), parts along dimension 0
There are 16 independent parts, one for each index of `dp`. A program takes and returns all parts, laid end to end along the dimension named above; an argument that names none is the same for every part. Nothing has to cross between parts.
All inputs are finite; a program needn't handle non-finite values.
Results may differ from a plain program's by a relative error of at most 0.01.
Values may be sent and summed in bfloat16 or wider, within the bound.
A program may use at most 128 MiB of HBM per device.

v0:
```python
import jax
import jax.numpy as jnp
from jax import lax
from jax.sharding import PartitionSpec as P

HEADS = 20
HEAD_SIZE = 128


def passed_along(value, axis, steps):
    count = lax.axis_size(axis)
    leading, last = (max(0, -steps), min(count, count - steps))
    return lax.ppermute(value, axis, [(source, source + steps) for source in range(leading, last)])


def attend_window(query_block, key_window, value_window, valid):
    block_rows = query_block.shape[0]
    window_rows = key_window.shape[0]
    query_heads = query_block.reshape(block_rows, HEADS, HEAD_SIZE)
    key_heads = key_window.reshape(window_rows, HEADS, HEAD_SIZE)
    value_heads = value_window.reshape(window_rows, HEADS, HEAD_SIZE)
    scores = jnp.einsum(
        "qhd,khd->hqk", query_heads, key_heads, preferred_element_type=jnp.float32
    ) * HEAD_SIZE ** (-0.5)
    scores = jnp.where(valid[None, None, :], scores, -1e30)
    largest = jnp.max(scores, axis=2, keepdims=True)
    expon = jnp.exp(scores - largest)
    probs = (expon / jnp.sum(expon, axis=2, keepdims=True)).astype(jnp.bfloat16)
    context = jnp.einsum("hqk,khd->qhd", probs, value_heads, preferred_element_type=jnp.float32)
    return context.astype(jnp.bfloat16).reshape(block_rows, HEADS * HEAD_SIZE)


def local(query_frames, key_frames, value_frames, stream, out_weight):
    block_rows = query_frames.shape[0]
    position = lax.axis_index("ctx")
    members = lax.axis_size("ctx")
    key_value = jnp.stack([key_frames, value_frames], 0)
    earlier = passed_along(key_value, "ctx", 1)
    later = passed_along(key_value, "ctx", -1)
    window = jnp.concatenate([earlier, key_value, later], 1)
    earlier_ok = jnp.broadcast_to(position > 0, (block_rows,))
    middle_ok = jnp.ones((block_rows,), dtype=bool)
    later_ok = jnp.broadcast_to(position < members - 1, (block_rows,))
    valid = jnp.concatenate([earlier_ok, middle_ok, later_ok])
    context = attend_window(query_frames, window[0], window[1], valid)
    product = jnp.dot(
        context,
        lax.all_gather(out_weight, "ctx", axis=0, tiled=True),
        preferred_element_type=jnp.float32,
    )
    return (stream.astype(jnp.float32) + product).astype(jnp.bfloat16)


def solution(mesh):
    in_specs = (
        P(("dp", "ctx"), None),
        P(("dp", "ctx"), None),
        P(("dp", "ctx"), None),
        P(("dp", "ctx"), None),
        P("ctx", None),
    )
    out_specs = P(("dp", "ctx"), None)
    return jax.shard_map(local, mesh=mesh, in_specs=in_specs, out_specs=out_specs, check_vma=False)
```

profile of v0, /device:TPU:1, one launch (start us, length us, event | category | flops | bytes accessed | tf_op | source)
XLA Modules:
  0.0 676.4 jit_solution(7607029471892932784)
XLA Ops:
  6.5 0.0 all-gather.2.cloned.1.call-start
  6.5 0.7 all-gather.2.cloned.1.call-update
  7.3 1.6 copy.9
  8.9 1.6 copy.10
  10.5 1.7 pad_maximum_fusion.1
  12.2 5.5 collective-permute-start
  17.7 1.3 collective-permute-start.1
  19.0 2.4 copy.11
  21.5 222.7 %collective-permute-done = bf16[2,256,2560]{1,2,0:T(8,128)(2,1)} collective-permute-done((bf16[2,256,2560]{1,2,0:T(8,128)(2,1)}, bf16[2,256,2560]{1,2,0:T(8,128)(2,1)}, u32[]{:S(2)}, u32[]{:S(2)}) %collective-permute-start) | collective-permute-done | bytes 2621472 | tf_op jit(solution)/shard_map/ppermute | solution.py:13
  244.2 0.0 collective-permute-done.1
  244.2 3.3 pad_maximum_fusion
  247.6 0.0 copy-start.1
  247.6 3.3 fusion.15
  250.9 0.0 copy-done.1
  250.9 10.6 %fusion.16 = (f32[20,256]{1,0:T(8,128)S(1)}, f32[20,256,768]{1,2,0:T(8,128)}) fusion(pred[768]{0:T(1024)(128)(4,1)S(1)} %pad_add_fusion, bf16[768,20,128]{0,2,1:T(8,128)(2,1)} %bitcast.31, bf16[256,20,128]{0,2,1:T(8,128)(2,1)S(1)} %bitcast.33), kind=kOutput, calls=%fused_computation.21 | convolution fusion | flops 1022362368 | bytes 20992768 | tf_op jit(solution)/shard_map/sub | solution.py:27
  261.5 0.0 copy-start
  261.5 9.3 %fusion.10 = bf16[20,128,256]{2,1,0:T(8,128)(2,1)} fusion(bf16[768,20,128]{0,2,1:T(8,128)(2,1)} %bitcast.30, f32[20,256,768]{1,2,0:T(8,128)} %get-tuple-element.8, f32[20,256]{1,0:T(8,128)S(1)} %get-tuple-element.7), kind=kOutput, calls=%fused_computation.15 | convolution fusion | flops 1015152640 | bytes 20992000 | tf_op jit(solution)/shard_map/hqk,khd->qhd/dot_general | solution.py:29
  270.8 385.2 %all-gather.2.cloned.1.call-done = bf16[2560,5120]{1,0:T(8,128)(2,1)} async-done(((bf16[160,5120]{1,0:T(8,128)(2,1)}), bf16[2560,5120]{1,0:T(8,128)(2,1)}) %all-gather.2.cloned.1.call-update) | async-done | bytes 26214416 | tf_op jit(solution)/shard_map/all_gather | solution.py:48
  656.1 0.0 copy-done
  656.1 13.5 %fusion.9 = bf16[256,5120]{1,0:T(8,128)(2,1)} fusion(bf16[256,2560]{0,1:T(8,128)(2,1)} %bitcast.32, bf16[2560,5120]{1,0:T(8,128)(2,1)} %all-gather.2.cloned.1.call-done, bf16[256,5120]{1,0:T(8,128)(2,1)S(1)} %copy-done), kind=kOutput, calls=%fused_computation.13 | convolution fusion | flops 6714818560 | bytes 32768000 | tf_op jit(solution)/shard_map/dot_general | solution.py:46
  (4 shorter events, 0.0 us)
Async XLA Ops:
  6.5 649.5 %all-gather.2.cloned.1.call-start = ((), (), s32[]{:S(2)}) async-start(), calls=%async_computation | async-start | bytes 27852800 | tf_op jit(solution)/shard_map/all_gather | solution.py:48
  12.2 232.0 %collective-permute-start = (bf16[2,256,2560]{1,2,0:T(8,128)(2,1)}, bf16[2,256,2560]{1,2,0:T(8,128)(2,1)}, u32[]{:S(2)}, u32[]{:S(2)}) collective-permute-start(bf16[2,256,2560]{1,2,0:T(8,128)(2,1)} %pad_maximum_fusion.1), channel_id=1, source_target_pairs={{0,1},{1,2},{2,3},{3,4},{4,5},{5,6},{6,7},{7,8},{8,9},{9,10},{10,1... | collective-permute-start | bytes 7864328 | tf_op jit(solution)/shard_map/ppermute | solution.py:13
  17.7 226.5 %collective-permute-start.1 = (bf16[2,256,2560]{1,2,0:T(8,128)(2,1)}, bf16[2,256,2560]{1,2,0:T(8,128)(2,1)}, u32[]{:S(2)}, u32[]{:S(2)}) collective-permute-start(bf16[2,256,2560]{1,2,0:T(8,128)(2,1)} %pad_maximum_fusion.1), channel_id=1, source_target_pairs={{1,0},{2,1},{3,2},{4,3},{5,4},{6,5},{7,6},{8,7},{9,8},{10,9},{11,1... | collective-permute-start | bytes 7864328 | tf_op jit(solution)/shard_map/ppermute | solution.py:13
  247.6 3.3 copy-start.1
  261.5 394.6 %copy-start = (bf16[256,5120]{1,0:T(8,128)(2,1)S(1)}, bf16[256,5120]{1,0:T(8,128)(2,1)}, u32[]{:S(2)}) copy-start(bf16[256,5120]{1,0:T(8,128)(2,1)} %param.8) | copy-start | bytes 7864324
Sparse Core Ops, SparseCore 0:
  9.1 646.9 all-gather.1
where the time goes:
time: 679 us; the launch traced here: 676 us
  waiting for transfers between devices  609 us (90%)
  matrix products  33.4 us (5%)
  between operations  13.5 us (2%)
  local copies, waits for them, and re-layouts  8.97 us (1%)
  starting transfers between devices  6.83 us (1%)
    all_gather x1, waiting for transfers between devices, local(): lax.all_gather(out_weight, 'ctx', axis=0, tiled=True)  385 us
    ppermute x2, waiting for transfers between devices, passed_along(): lax.ppermute(value, axis, [(source, source + steps) for source in range(l...  223 us
  transfers between devices with their start and end apart: 3, of which 2 were waited for; matrix products, arithmetic and copies ran while one was open for 5% of the time, Pallas kernels for 0%

commit v1 on v0

v1 whole, which is shorter than its diff:
```python
import jax
import jax.numpy as jnp
from jax import lax
from jax.experimental import pallas as pl
from jax.experimental.pallas import tpu as pltpu
from jax.sharding import PartitionSpec as P

HEADS = 20
HEAD_SIZE = 128
BLOCK = 256
WIDTH = 2560
D = 5120
SHARD = 160
ROWS = 80
COLS = 1280
GROUPS = 10
TICKS = 14
SCALE = HEAD_SIZE ** (-0.5) * 1.4426950408889634
MESH = pl.DeviceIdType.MESH


def kernel(
    q_hbm, k_hbm, v_hbm, stream_hbm, w_hbm, out_hbm,
    q, own, near, far, ctx, stream, weight, out,
    in_sem, z_send, z_recv, h_send, h_recv, y_send, y_recv, x_send, x_recv,
    d_send, d_recv, c_send, c_recv, near_send, near_recv, far_send, far_recv, out_sem,
):
    dp = lax.axis_index("dp")
    at = lax.axis_index("ctx")
    core = lax.rem(dp, 2)
    x = lax.div(dp, 4)
    y_hi = lax.rem(lax.div(dp, 2), 2)
    z = lax.div(at, 2)
    par = lax.rem(at, 2)
    sig = 1 - 2 * par
    mine = lax.rem(x, 2)

    def plane(step):
        return lax.rem(z + step + 16, 8)

    z_out = (dp, plane(-sig) * 2 + par)
    h_out = (dp, plane(sig) * 2 + par)
    y_far = (dp + 2 - 4 * y_hi, at + 1 - 2 * par)
    y_near = (dp, at + 1 - 2 * par)
    other = (dp + 1 - 2 * core, at)

    def x_dev(r):
        return (lax.rem(dp + 4 + 8 * r, 16), at)

    barrier = pltpu.get_barrier_semaphore()
    for dev in (z_out, h_out, y_far, y_near, other, x_dev(0), x_dev(1)):
        pl.semaphore_signal(barrier, inc=1, device_id=dev, device_id_type=MESH)
    pl.semaphore_wait(barrier, 7)

    def piece(parity, zz, half, r):
        row = pl.multiple_of(SHARD * (2 * zz + parity) + ROWS * r, 16)
        col = pl.multiple_of(core * WIDTH + half * COLS, COLS)
        return weight.at[pl.ds(row, ROWS), pl.ds(col, COLS)]

    def source(half, r):
        row = pl.multiple_of(ROWS * r, 16)
        col = pl.multiple_of(core * WIDTH + half * COLS, COLS)
        return w_hbm.at[pl.ds(row, ROWS), pl.ds(col, COLS)]

    def remote(src, dst, send, recv, dev):
        return pltpu.make_async_remote_copy(
            src_ref=src, dst_ref=dst, send_sem=send, recv_sem=recv, device_id=dev, device_id_type=MESH
        )

    def spot(parity, zz, r):
        return piece(parity, zz, mine, r)

    def z_spot(t, half):
        early = t < 12
        step = jnp.where(early, sig * (1 + lax.div(t, 2)), -6 * sig)
        return piece(jnp.where(early, par, 1 - par), plane(step), half, lax.rem(t, 2))

    def h_spot(t, half):
        return piece(par, plane(-sig), half, 1 - t)

    def y_spot(t, half):
        n = lax.div(t, 2)
        k = jnp.where(n == 0, 0, jnp.where(n == 1, 7, n - 1))
        return piece(1 - par, plane(-sig * k), half, 1 - lax.rem(t, 2))

    def x_spot(r, t, half):
        by_z = lax.rem(t, 2) == r
        n = lax.div(t, 2)
        z_step = jnp.where(t < 12, sig * (1 + n), -6 * sig)
        y_step = jnp.where(t < 2, -sig, -sig * jnp.where(n == 1, 7, n - 1))
        z_par = jnp.where(t < 12, par, 1 - par)
        y_par = jnp.where(t < 2, par, 1 - par)
        return piece(jnp.where(by_z, z_par, y_par), plane(jnp.where(by_z, z_step, y_step)), half, r)

    def pass_over(ref, i):
        remote(ref, ref, c_send.at[i], c_recv.at[i], other).start()

    def arrived(ref, send, recv):
        remote(ref, ref, send, recv, other).wait_recv()

    def kv(ref_k, ref_v, which, g):
        cols = pl.ds(pl.multiple_of(g * 256, 256), 256)
        return (ref_k if which == 0 else ref_v).at[:, cols]

    def slot(buf, which, g):
        return buf.at[which, :, pl.ds(pl.multiple_of(g * 256, 256), 256)]

    def start_near(g):
        for which in range(2):
            remote(
                kv(k_hbm, v_hbm, which, g), slot(near, which, g),
                near_send.at[which, g], near_recv.at[which, g], y_near,
            ).start()

    start_near(0)
    for i in range(2):
        home = piece(par, z, mine, i)
        remote(source(mine, i), home, z_send.at[i], z_recv.at[i], z_out).start()
        home = piece(par, z, mine, 1 - i)
        remote(source(mine, 1 - i), home, h_send.at[i], h_recv.at[i], h_out).start()
        remote(source(mine, 1 - i), home, y_send.at[i], y_recv.at[i], y_far).start()

    @pl.loop(1, GROUPS)
    def _(g):
        start_near(g)

    for i in range(2):
        home = piece(par, z, 1 - mine, i)
        remote(source(1 - mine, i), home, d_send.at[i], d_recv.at[i], y_near).start()

    loads = [
        pltpu.make_async_copy(q_hbm, q, in_sem.at[0]),
        pltpu.make_async_copy(k_hbm, own.at[0], in_sem.at[1]),
        pltpu.make_async_copy(v_hbm, own.at[1], in_sem.at[2]),
        pltpu.make_async_copy(
            w_hbm, weight.at[pl.ds(pl.multiple_of(SHARD * at, 16), SHARD), :], in_sem.at[3]
        ),
        pltpu.make_async_copy(stream_hbm, stream, in_sem.at[4]),
    ]
    for load in loads:
        load.start()
    for load in loads:
        load.wait()

    bias = jnp.where((z + par > 0) & (z + par < 8), 0.0, -1e30).astype(jnp.float32)
    ones = jnp.ones((BLOCK, HEAD_SIZE), jnp.bfloat16)

    def attend(h):
        cols = pl.ds(pl.multiple_of(h * HEAD_SIZE, HEAD_SIZE), HEAD_SIZE)
        query = q[:, cols]

        def score(buf):
            return lax.dot_general(
                query, buf[0, :, cols], (((1,), (1,)), ((), ())), preferred_element_type=jnp.float32
            )

        scores = [score(own), score(near), score(far) + bias]
        largest = jnp.maximum(jnp.maximum(scores[0], scores[1]), scores[2]).max(axis=1, keepdims=True)
        total = None
        for buf, s in zip((own, near, far), scores):
            expon = jnp.exp2((s - largest) * SCALE).astype(jnp.bfloat16)
            values = jnp.concatenate([buf[1, :, cols], ones], axis=1)
            part = jnp.dot(expon, values, preferred_element_type=jnp.float32)
            total = part if total is None else total + part
        ctx[:, cols] = (total[:, :HEAD_SIZE] / total[:, HEAD_SIZE:]).astype(jnp.bfloat16)

    @pl.loop(0, TICKS + 1)
    def _(t):
        @pl.when(t < TICKS)
        def _():
            got = z_spot(t, mine)
            arrived(got, z_send.at[t], z_recv.at[t])

            @pl.when(t < 12)
            def _():
                k = jnp.where(t < 10, sig * (1 + lax.div(t, 2)), -7 * sig)
                ref = spot(jnp.where(t < 10, par, 1 - par), plane(k), lax.rem(t, 2))
                remote(ref, ref, z_send.at[t + 2], z_recv.at[t + 2], z_out).start()

            r = lax.rem(t, 2)
            remote(got, got, x_send.at[r, t], x_recv.at[r, t], x_dev(r)).start()
            pass_over(got, t)

            @pl.when(t < 2)
            def _():
                ref = h_spot(t, mine)
                arrived(ref, h_send.at[t], h_recv.at[t])
                remote(ref, ref, x_send.at[1 - r, t], x_recv.at[1 - r, t], x_dev(1 - r)).start()
                remote(ref, ref, y_send.at[t + 2], y_recv.at[t + 2], y_far).start()
                pass_over(ref, 14 + t)

            @pl.when((t > 0) & (t < 11))
            def _():
                ref = spot(par, plane(sig * (lax.div(t + 3, 2) - 1)), r)
                remote(ref, ref, y_send.at[t + 3], y_recv.at[t + 3], y_far).start()

            ref = y_spot(t, mine)
            arrived(ref, y_send.at[t], y_recv.at[t])

            @pl.when(t >= 2)
            def _():
                remote(ref, ref, x_send.at[1 - r, t], x_recv.at[1 - r, t], x_dev(1 - r)).start()

            pass_over(ref, 16 + t)

        @pl.loop(lax.div(t * 25, 32), jnp.minimum(lax.div((t + 1) * 25, 32), GROUPS))
        def _(g):
            for which in range(2):
                ref = slot(near, which, g)
                arrived(ref, near_send.at[which, g], near_recv.at[which, g])
                remote(ref, slot(far, which, g), far_send.at[which, g], far_recv.at[which, g], h_out).start()

        @pl.when(t >= 1)
        def _():
            for r in range(2):
                ref = x_spot(r, t - 1, 1 - mine)
                arrived(ref, x_send.at[r, t - 1], x_recv.at[r, t - 1])
                pass_over(ref, 30 + r * 14 + t - 1)

        def ready(s):
            return lax.div(jnp.maximum(s - 2, 0) * 25, 32)

        @pl.loop(ready(t), jnp.minimum(ready(t + 1), GROUPS))
        def _(g):
            for which in range(2):
                arrived(slot(far, which, g), far_send.at[which, g], far_recv.at[which, g])

            @pl.loop(0, 2)
            def _(i):
                attend(2 * g + i)

    for i in range(2):
        ref = piece(1 - par, z, 1 - mine, i)
        arrived(ref, d_send.at[i], d_recv.at[i])
        pass_over(ref, 58 + i)

    any_piece = weight.at[pl.ds(0, ROWS), pl.ds(0, COLS)]

    @pl.loop(0, 60)
    def _(i):
        arrived(any_piece, c_send.at[i], c_recv.at[i])

    def out_copy(n):
        cols = pl.ds(pl.multiple_of(n * 512, 512), 512)
        return pltpu.make_async_copy(out.at[:, cols], out_hbm.at[:, cols], out_sem.at[n])

    @pl.loop(0, 10)
    def _(n):
        cols = pl.ds(pl.multiple_of(n * 512, 512), 512)
        product = jnp.dot(ctx[...], weight[:, cols], preferred_element_type=jnp.float32)
        out[:, cols] = (stream[:, cols].astype(jnp.float32) + product).astype(jnp.bfloat16)
        out_copy(n).start()

    def sent(ref, send, recv):
        remote(ref, ref, send, recv, other).wait_send()

    @pl.loop(0, 14)
    def _(i):
        sent(any_piece, z_send.at[i], z_recv.at[i])
        sent(any_piece, y_send.at[i], y_recv.at[i])
        for r in range(2):
            sent(any_piece, x_send.at[r, i], x_recv.at[r, i])

    for i in range(2):
        sent(any_piece, h_send.at[i], h_recv.at[i])
        sent(any_piece, d_send.at[i], d_recv.at[i])

    @pl.loop(0, 60)
    def _(i):
        sent(any_piece, c_send.at[i], c_recv.at[i])

    @pl.loop(0, GROUPS)
    def _(g):
        for which in range(2):
            sent(slot(near, which, g), near_send.at[which, g], near_recv.at[which, g])
            sent(slot(far, which, g), far_send.at[which, g], far_recv.at[which, g])
        out_copy(g).wait()


def local(query_frames, key_frames, value_frames, stream, out_weight):
    dma = pltpu.SemaphoreType.DMA
    bf16 = jnp.bfloat16
    return pl.pallas_call(
        kernel,
        out_shape=jax.ShapeDtypeStruct((BLOCK, D), bf16),
        in_specs=[pl.BlockSpec(memory_space=pl.ANY)] * 5,
        out_specs=pl.BlockSpec(memory_space=pl.ANY),
        scratch_shapes=[
            pltpu.VMEM((BLOCK, WIDTH), bf16),
            pltpu.VMEM((2, BLOCK, WIDTH), bf16),
            pltpu.VMEM((2, BLOCK, WIDTH), bf16),
            pltpu.VMEM((2, BLOCK, WIDTH), bf16),
            pltpu.VMEM((BLOCK, WIDTH), bf16),
            pltpu.VMEM((BLOCK, D), bf16),
            pltpu.VMEM((WIDTH, D), bf16),
            pltpu.VMEM((BLOCK, D), bf16),
            dma((5,)),
            dma((14,)), dma((14,)),
            dma((2,)), dma((2,)),
            dma((14,)), dma((14,)),
            dma((2, 14)), dma((2, 14)),
            dma((2,)), dma((2,)),
            dma((60,)), dma((60,)),
            dma((2, GROUPS)), dma((2, GROUPS)),
            dma((2, GROUPS)), dma((2, GROUPS)),
            dma((10,)),
        ],
        compiler_params=pltpu.CompilerParams(
            collective_id=0, has_side_effects=True, vmem_limit_bytes=63 * 1024 * 1024
        ),
    )(query_frames, key_frames, value_frames, stream, out_weight)


def solution(mesh):
    in_specs = (
        P(("dp", "ctx"), None),
        P(("dp", "ctx"), None),
        P(("dp", "ctx"), None),
        P(("dp", "ctx"), None),
        P("ctx", None),
    )
    out_specs = P(("dp", "ctx"), None)
    return jax.shard_map(local, mesh=mesh, in_specs=in_specs, out_specs=out_specs, check_vma=False)
```

time: 679 us -> 98.8 us (0.15)
  waiting for transfers between devices: 609 us -> 0 us
  Pallas kernels: 0 us -> 95.3 us
  matrix products: 33.4 us -> 0 us
  between operations: 13.5 us -> 0.01 us
  starting transfers between devices: 6.83 us -> 0 us
    all_gather x1 -> x0, waiting for transfers between devices: 385 us -> none  [local(): lax.all_gather(out_weight, 'ctx', axis=0, tiled=True)]
    ppermute x2 -> x0, waiting for transfers between devices: 223 us -> none  [passed_along(): lax.ppermute(value, axis, [(source, source + steps) for source in range(l...]
    pallas_call x0 -> x1, Pallas kernels: none -> 95.3 us  [local(): pl.pallas_call(kernel, out_shape=jax.ShapeDtypeStruct((BLOCK, D), bf16),...]
    dot_general x2 -> x0, matrix products: 22.8 us -> none  [the longest x1 13.5 us: local(): jnp.dot(context, lax.all_gather(out_weight, 'ctx', axis=0, tiled=True), p...]
    sub x1 -> x0, matrix products: 10.6 us -> none  [attend_window(): expon = jnp.exp(scores - largest)]
    ppermute x2 -> x0, starting transfers between devices: 6.83 us -> none  [passed_along(): lax.ppermute(value, axis, [(source, source + steps) for source in range(l...]
  transfers between devices with their start and end apart: 3 -> 0, of which waited for: 2 -> 0; matrix products, arithmetic and copies ran while one was open for 5% -> 0% of each run, Pallas kernels for 0% -> 0%
where the time goes in v1:
time: 98.8 us; the launch traced here: 98.7 us
  Pallas kernels  95.3 us (96%)
  local copies, waits for them, and re-layouts  3.4 us (3%)
    pallas_call x1, Pallas kernels, local(): pl.pallas_call(kernel, out_shape=jax.ShapeDtypeStruct((BLOCK, D), bf16),...  95.3 us
    unnamed x1, local copies, waits for them, and re-layouts  3.4 us

profile of v1, /device:TPU:1, one launch (start us, length us, event | category | flops | bytes accessed | tf_op | source)
XLA Modules:
  0.0 98.7 jit_solution(11340259151134445961)
XLA Ops:
  0.0 95.3 %shard_map.55 = bf16[256,5120]{1,0:T(8,128)(2,1)} custom-call(bf16[256,2560]{1,0:T(8,128)(2,1)} %q_hbm.1, bf16[256,2560]{1,0:T(8,128)(2,1)} %k_hbm.1, bf16[256,2560]{1,0:T(8,128)(2,1)} %v_hbm.1, bf16[256,5120]{1,0:T(8,128)(2,1)} %stream_hbm.1, bf16[160,5120]{1,0:T(8,128)(2,1)} %w_hbm.1), custom_call_target="tpu_custom_call" | custom-call | tf_op jit(solution)/shard_map/pallas_call | solution.py:283
  95.3 3.4 %copy.7 = bf16[256,5120]{1,0:T(8,128)(2,1)} copy(bf16[256,5120]{1,0:T(8,128)(2,1)} %shard_map.55) | data formatting | bytes 5242880

commit v2 on v1

--- a/solution.py
+++ b/solution.py
@@ -15,15 +15,16 @@
 COLS = 1280
 GROUPS = 10
 TICKS = 14
+LAST = 15
 SCALE = HEAD_SIZE ** (-0.5) * 1.4426950408889634
 MESH = pl.DeviceIdType.MESH
 
 
 def kernel(
-    q_hbm, k_hbm, v_hbm, stream_hbm, w_hbm, out_hbm,
-    q, own, near, far, ctx, stream, weight, out,
+    q_hbm, k_hbm, v_hbm, stream_hbm, w_hbm, out,
+    q, own, near, far, ctx, stream, weight, total,
     in_sem, z_send, z_recv, h_send, h_recv, y_send, y_recv, x_send, x_recv,
-    d_send, d_recv, c_send, c_recv, near_send, near_recv, far_send, far_recv, out_sem,
+    d_send, d_recv, c_send, c_recv, near_send, near_recv, far_send, far_recv,
 ):
     dp = lax.axis_index("dp")
     at = lax.axis_index("ctx")
@@ -123,10 +124,6 @@
     @pl.loop(1, GROUPS)
     def _(g):
         start_near(g)
-
-    for i in range(2):
-        home = piece(par, z, 1 - mine, i)
-        remote(source(1 - mine, i), home, d_send.at[i], d_recv.at[i], y_near).start()
 
     loads = [
         pltpu.make_async_copy(q_hbm, q, in_sem.at[0]),
@@ -141,6 +138,8 @@
         load.start()
     for load in loads:
         load.wait()
+    total[...] = stream[...].astype(jnp.float32)
+    any_piece = weight.at[pl.ds(0, ROWS), pl.ds(0, COLS)]
 
     bias = jnp.where((z + par > 0) & (z + par < 8), 0.0, -1e30).astype(jnp.float32)
     ones = jnp.ones((BLOCK, HEAD_SIZE), jnp.bfloat16)
@@ -156,15 +155,53 @@
 
         scores = [score(own), score(near), score(far) + bias]
         largest = jnp.maximum(jnp.maximum(scores[0], scores[1]), scores[2]).max(axis=1, keepdims=True)
-        total = None
+        summed = None
         for buf, s in zip((own, near, far), scores):
             expon = jnp.exp2((s - largest) * SCALE).astype(jnp.bfloat16)
             values = jnp.concatenate([buf[1, :, cols], ones], axis=1)
             part = jnp.dot(expon, values, preferred_element_type=jnp.float32)
-            total = part if total is None else total + part
-        ctx[:, cols] = (total[:, :HEAD_SIZE] / total[:, HEAD_SIZE:]).astype(jnp.bfloat16)
-
-    @pl.loop(0, TICKS + 1)
+            summed = part if summed is None else summed + part
+        ctx[:, cols] = (summed[:, :HEAD_SIZE] / summed[:, HEAD_SIZE:]).astype(jnp.bfloat16)
+
+    def accumulate(row, depth):
+        rows = pl.ds(pl.multiple_of(row, HEAD_SIZE), depth)
+
+        @pl.loop(0, D // COLS)
+        def _(n):
+            cols = pl.ds(pl.multiple_of(n * COLS, COLS), COLS)
+            total[:, cols] += jnp.dot(ctx[:, rows], weight[rows, cols], preferred_element_type=jnp.float32)
+
+    def first_row(zz):
+        return 640 * lax.div(zz, 2) + 384 * lax.rem(zz, 2)
+
+    def due(zz):
+        m = lax.rem(sig * (zz - z) + 16, 8)
+        rows_here = jnp.where(m == 0, 4, jnp.where(m == 1, 6, jnp.where(m < 4, LAST, 14)))
+        rows_here = jnp.where(m == 5, 12, jnp.where(m == 7, 8, rows_here))
+        heads_here = jnp.where(zz < 4, jnp.where(zz < 2, 3 + 2 * zz, 5 + zz), jnp.where(zz < 5, 9, 7 + zz))
+        return jnp.maximum(rows_here, heads_here)
+
+    def project(t):
+        @pl.loop(0, 4)
+        def _(j):
+            lower, upper = due(2 * j), due(2 * j + 1)
+
+            @pl.when(lower == t)
+            def _():
+                accumulate(640 * j, 256)
+
+            @pl.when(upper == t)
+            def _():
+                accumulate(640 * j + 384, 256)
+
+            @pl.when(jnp.maximum(lower, upper) == t)
+            def _():
+                accumulate(640 * j + 256, 128)
+
+    def handed(i):
+        arrived(any_piece, c_send.at[i], c_recv.at[i])
+
+    @pl.loop(0, LAST)
     def _(t):
         @pl.when(t < TICKS)
         def _():
@@ -178,7 +215,11 @@
                 remote(ref, ref, z_send.at[t + 2], z_recv.at[t + 2], z_out).start()
 
             r = lax.rem(t, 2)
-            remote(got, got, x_send.at[r, t], x_recv.at[r, t], x_dev(r)).start()
+
+            @pl.when(t < 13)
+            def _():
+                remote(got, got, x_send.at[r, t], x_recv.at[r, t], x_dev(r)).start()
+
             pass_over(got, t)
 
             @pl.when(t < 2)
@@ -197,9 +238,10 @@
             ref = y_spot(t, mine)
             arrived(ref, y_send.at[t], y_recv.at[t])
 
-            @pl.when(t >= 2)
-            def _():
-                remote(ref, ref, x_send.at[1 - r, t], x_recv.at[1 - r, t], x_dev(1 - r)).start()
+            @pl.when(t < 13)
+            def _():
+                i = jnp.where(t < 2, 13, t)
+                remote(ref, ref, x_send.at[1 - r, i], x_recv.at[1 - r, i], x_dev(1 - r)).start()
 
             pass_over(ref, 16 + t)
 
@@ -210,12 +252,29 @@
                 arrived(ref, near_send.at[which, g], near_recv.at[which, g])
                 remote(ref, slot(far, which, g), far_send.at[which, g], far_recv.at[which, g], h_out).start()
 
-        @pl.when(t >= 1)
+        @pl.when(t >= 2)
         def _():
             for r in range(2):
-                ref = x_spot(r, t - 1, 1 - mine)
-                arrived(ref, x_send.at[r, t - 1], x_recv.at[r, t - 1])
-                pass_over(ref, 30 + r * 14 + t - 1)
+                ref = x_spot(r, t - 2, 1 - mine)
+                arrived(ref, x_send.at[r, t - 2], x_recv.at[r, t - 2])
+                pass_over(ref, 30 + r * 13 + t - 2)
+
+        @pl.when(t == 3)
+        def _():
+            for r in range(2):
+                ref = piece(1 - par, z, 1 - mine, r)
+                arrived(ref, x_send.at[r, 13], x_recv.at[r, 13])
+                pass_over(ref, 56 + r)
+
+        @pl.when(t == 10)
+        def _():
+            ref = piece(par, plane(5 * sig), 1 - mine, 0)
+            remote(ref, ref, d_send.at[0], d_recv.at[0], y_near).start()
+
+        @pl.when(t == 13)
+        def _():
+            ref = piece(par, plane(6 * sig), 1 - mine, 1)
+            remote(ref, ref, d_send.at[1], d_recv.at[1], y_near).start()
 
         def ready(s):
             return lax.div(jnp.maximum(s - 2, 0) * 25, 32)
@@ -229,27 +288,50 @@
             def _(i):
                 attend(2 * g + i)
 
+        @pl.when(t >= 1)
+        def _():
+            handed(t - 1)
+            handed(16 + t - 1)
+
+        @pl.when((t == 1) | (t == 2))
+        def _():
+            handed(14 + t - 1)
+
+        @pl.when(t >= 3)
+        def _():
+            handed(30 + t - 3)
+            handed(43 + t - 3)
+
+        @pl.when(t == 4)
+        def _():
+            handed(56)
+            handed(57)
+
+        project(t)
+
     for i in range(2):
-        ref = piece(1 - par, z, 1 - mine, i)
+        ref = piece(1 - par, plane(-(5 + i) * sig), 1 - mine, i)
         arrived(ref, d_send.at[i], d_recv.at[i])
         pass_over(ref, 58 + i)
 
-    any_piece = weight.at[pl.ds(0, ROWS), pl.ds(0, COLS)]
-
-    @pl.loop(0, 60)
-    def _(i):
-        arrived(any_piece, c_send.at[i], c_recv.at[i])
-
-    def out_copy(n):
-        cols = pl.ds(pl.multiple_of(n * 512, 512), 512)
-        return pltpu.make_async_copy(out.at[:, cols], out_hbm.at[:, cols], out_sem.at[n])
-
-    @pl.loop(0, 10)
+    for i in (42, 55, 58, 59):
+        handed(i)
+
+    @pl.loop(0, 4)
+    def _(j):
+        @pl.when(jnp.maximum(due(2 * j), due(2 * j + 1)) == LAST)
+        def _():
+            accumulate(640 * j + 256, 128)
+
+    ends = [pl.ds(pl.multiple_of(first_row(plane(m * sig)), HEAD_SIZE), 256) for m in (2, 3)]
+
+    @pl.loop(0, D // COLS)
     def _(n):
-        cols = pl.ds(pl.multiple_of(n * 512, 512), 512)
-        product = jnp.dot(ctx[...], weight[:, cols], preferred_element_type=jnp.float32)
-        out[:, cols] = (stream[:, cols].astype(jnp.float32) + product).astype(jnp.bfloat16)
-        out_copy(n).start()
+        cols = pl.ds(pl.multiple_of(n * COLS, COLS), COLS)
+        product = total[:, cols]
+        for rows in ends:
+            product += jnp.dot(ctx[:, rows], weight[rows, cols], preferred_element_type=jnp.float32)
+        out[:, cols] = product.astype(jnp.bfloat16)
 
     def sent(ref, send, recv):
         remote(ref, ref, send, recv, other).wait_send()
@@ -274,7 +356,6 @@
         for which in range(2):
             sent(slot(near, which, g), near_send.at[which, g], near_recv.at[which, g])
             sent(slot(far, which, g), far_send.at[which, g], far_recv.at[which, g])
-        out_copy(g).wait()
 
 
 def local(query_frames, key_frames, value_frames, stream, out_weight):
@@ -283,8 +364,8 @@
     return pl.pallas_call(
         kernel,
         out_shape=jax.ShapeDtypeStruct((BLOCK, D), bf16),
-        in_specs=[pl.BlockSpec(memory_space=pl.ANY)] * 5,
-        out_specs=pl.BlockSpec(memory_space=pl.ANY),
+        in_specs=[pl.BlockSpec(memory_space=pltpu.HBM)] * 5,
+        out_specs=pl.BlockSpec(memory_space=pltpu.VMEM),
         scratch_shapes=[
             pltpu.VMEM((BLOCK, WIDTH), bf16),
             pltpu.VMEM((2, BLOCK, WIDTH), bf16),
@@ -293,7 +374,7 @@
             pltpu.VMEM((BLOCK, WIDTH), bf16),
             pltpu.VMEM((BLOCK, D), bf16),
             pltpu.VMEM((WIDTH, D), bf16),
-            pltpu.VMEM((BLOCK, D), bf16),
+            pltpu.VMEM((BLOCK, D), jnp.float32),
             dma((5,)),
             dma((14,)), dma((14,)),
             dma((2,)), dma((2,)),
@@ -303,12 +384,11 @@
             dma((60,)), dma((60,)),
             dma((2, GROUPS)), dma((2, GROUPS)),
             dma((2, GROUPS)), dma((2, GROUPS)),
-            dma((10,)),
         ],
         compiler_params=pltpu.CompilerParams(
-            collective_id=0, has_side_effects=True, vmem_limit_bytes=63 * 1024 * 1024
+            collective_id=0, has_side_effects=True, vmem_limit_bytes=50 * 1024 * 1024
         ),
-    )(query_frames, key_frames, value_frames, stream, out_weight)
+    )(*[pltpu.with_memory_space_constraint(a, pltpu.HBM) for a in (query_frames, key_frames, value_frames, stream, out_weight)])
 
 
 def solution(mesh):

time: 98.8 us -> 97.6 us (0.988)
  local copies, waits for them, and re-layouts: 3.4 us -> 1.49 us
    unnamed x1, local copies, waits for them, and re-layouts: 3.4 us -> 1.49 us
where the time goes in v2:
time: 97.6 us; the launch traced here: 97.5 us
  Pallas kernels  96 us (98%)
  local copies, waits for them, and re-layouts  1.49 us (2%)
    pallas_call x1, Pallas kernels, local(): pl.pallas_call(kernel, out_shape=jax.ShapeDtypeStruct((BLOCK, D), bf16),...  96 us

profile of v2, /device:TPU:1, one launch (start us, length us, event | category | flops | bytes accessed | tf_op | source)
XLA Modules:
  0.0 97.5 jit_solution(481035286504911585)
XLA Ops:
  0.0 96.0 %shard_map.55 = bf16[256,5120]{1,0:T(8,128)(2,1)S(1)} custom-call(bf16[256,2560]{1,0:T(8,128)(2,1)} %q_hbm.1, bf16[256,2560]{1,0:T(8,128)(2,1)} %k_hbm.1, bf16[256,2560]{1,0:T(8,128)(2,1)} %v_hbm.1, bf16[256,5120]{1,0:T(8,128)(2,1)} %stream_hbm.1, bf16[160,5120]{1,0:T(8,128)(2,1)} %w_hbm.1), custom_call_target="tpu_custom_call" | custom-call | tf_op jit(solution)/shard_map/pallas_call | solution.py:364
  96.0 1.5 %copy.7 = bf16[256,5120]{1,0:T(8,128)(2,1)} copy(bf16[256,5120]{1,0:T(8,128)(2,1)S(1)} %shard_map.55) | data formatting | bytes 5242880

commit v3 on v2

--- a/solution.py
+++ b/solution.py
@@ -15,14 +15,13 @@
 COLS = 1280
 GROUPS = 10
 TICKS = 14
-LAST = 15
 SCALE = HEAD_SIZE ** (-0.5) * 1.4426950408889634
 MESH = pl.DeviceIdType.MESH
 
 
 def kernel(
-    q_hbm, k_hbm, v_hbm, stream_hbm, w_hbm, out,
-    q, own, near, far, ctx, stream, weight, total,
+    q_hbm, k_hbm, v_hbm, stream_hbm, w_hbm, total,
+    q, own, near, far, ctx, stream, weight,
     in_sem, z_send, z_recv, h_send, h_recv, y_send, y_recv, x_send, x_recv,
     d_send, d_recv, c_send, c_recv, near_send, near_recv, far_send, far_recv,
 ):
@@ -163,22 +162,27 @@
             summed = part if summed is None else summed + part
         ctx[:, cols] = (summed[:, :HEAD_SIZE] / summed[:, HEAD_SIZE:]).astype(jnp.bfloat16)
 
+    def attend_group(g):
+        for which in range(2):
+            arrived(slot(far, which, g), far_send.at[which, g], far_recv.at[which, g])
+
+        @pl.loop(0, 2)
+        def _(i):
+            attend(2 * g + i)
+
     def accumulate(row, depth):
         rows = pl.ds(pl.multiple_of(row, HEAD_SIZE), depth)
 
-        @pl.loop(0, D // COLS)
+        @pl.loop(0, D // WIDTH)
         def _(n):
-            cols = pl.ds(pl.multiple_of(n * COLS, COLS), COLS)
+            cols = pl.ds(pl.multiple_of(n * WIDTH, WIDTH), WIDTH)
             total[:, cols] += jnp.dot(ctx[:, rows], weight[rows, cols], preferred_element_type=jnp.float32)
-
-    def first_row(zz):
-        return 640 * lax.div(zz, 2) + 384 * lax.rem(zz, 2)
 
     def due(zz):
         m = lax.rem(sig * (zz - z) + 16, 8)
-        rows_here = jnp.where(m == 0, 4, jnp.where(m == 1, 6, jnp.where(m < 4, LAST, 14)))
-        rows_here = jnp.where(m == 5, 12, jnp.where(m == 7, 8, rows_here))
-        heads_here = jnp.where(zz < 4, jnp.where(zz < 2, 3 + 2 * zz, 5 + zz), jnp.where(zz < 5, 9, 7 + zz))
+        rows_here = jnp.where(m == 0, 3, jnp.where(m == 1, 5, jnp.where(m < 4, TICKS, 13)))
+        rows_here = jnp.where(m == 5, 11, jnp.where(m == 7, 7, rows_here))
+        heads_here = jnp.where(zz < 4, jnp.where(zz < 1, 3, 5 + zz), jnp.where(zz < 5, 9, 7 + zz))
         return jnp.maximum(rows_here, heads_here)
 
     def project(t):
@@ -186,107 +190,118 @@
         def _(j):
             lower, upper = due(2 * j), due(2 * j + 1)
 
-            @pl.when(lower == t)
+            @pl.when((lower == t) & (upper == t))
+            def _():
+                accumulate(640 * j, 640)
+
+            @pl.when((lower == t) & (upper > t))
             def _():
                 accumulate(640 * j, 256)
 
-            @pl.when(upper == t)
+            @pl.when((lower == t) & (upper < t))
+            def _():
+                accumulate(640 * j, 384)
+
+            @pl.when((upper == t) & (lower > t))
             def _():
                 accumulate(640 * j + 384, 256)
 
-            @pl.when(jnp.maximum(lower, upper) == t)
+            @pl.when((upper == t) & (lower < t))
             def _():
-                accumulate(640 * j + 256, 128)
+                accumulate(640 * j + 256, 384)
 
     def handed(i):
         arrived(any_piece, c_send.at[i], c_recv.at[i])
 
-    @pl.loop(0, LAST)
+    @pl.loop(0, TICKS)
     def _(t):
-        @pl.when(t < TICKS)
-        def _():
-            got = z_spot(t, mine)
-            arrived(got, z_send.at[t], z_recv.at[t])
-
-            @pl.when(t < 12)
-            def _():
-                k = jnp.where(t < 10, sig * (1 + lax.div(t, 2)), -7 * sig)
-                ref = spot(jnp.where(t < 10, par, 1 - par), plane(k), lax.rem(t, 2))
-                remote(ref, ref, z_send.at[t + 2], z_recv.at[t + 2], z_out).start()
-
-            r = lax.rem(t, 2)
-
-            @pl.when(t < 13)
-            def _():
-                remote(got, got, x_send.at[r, t], x_recv.at[r, t], x_dev(r)).start()
-
-            pass_over(got, t)
-
-            @pl.when(t < 2)
-            def _():
-                ref = h_spot(t, mine)
-                arrived(ref, h_send.at[t], h_recv.at[t])
-                remote(ref, ref, x_send.at[1 - r, t], x_recv.at[1 - r, t], x_dev(1 - r)).start()
-                remote(ref, ref, y_send.at[t + 2], y_recv.at[t + 2], y_far).start()
-                pass_over(ref, 14 + t)
-
-            @pl.when((t > 0) & (t < 11))
-            def _():
-                ref = spot(par, plane(sig * (lax.div(t + 3, 2) - 1)), r)
-                remote(ref, ref, y_send.at[t + 3], y_recv.at[t + 3], y_far).start()
-
-            ref = y_spot(t, mine)
-            arrived(ref, y_send.at[t], y_recv.at[t])
-
-            @pl.when(t < 13)
-            def _():
-                i = jnp.where(t < 2, 13, t)
-                remote(ref, ref, x_send.at[1 - r, i], x_recv.at[1 - r, i], x_dev(1 - r)).start()
-
-            pass_over(ref, 16 + t)
-
-        @pl.loop(lax.div(t * 25, 32), jnp.minimum(lax.div((t + 1) * 25, 32), GROUPS))
+        got = z_spot(t, mine)
+        arrived(got, z_send.at[t], z_recv.at[t])
+
+        @pl.when(t < 12)
+        def _():
+            k = jnp.where(t < 10, sig * (1 + lax.div(t, 2)), -7 * sig)
+            ref = spot(jnp.where(t < 10, par, 1 - par), plane(k), lax.rem(t, 2))
+            remote(ref, ref, z_send.at[t + 2], z_recv.at[t + 2], z_out).start()
+
+        r = lax.rem(t, 2)
+
+        @pl.when(t < 13)
+        def _():
+            remote(got, got, x_send.at[r, t], x_recv.at[r, t], x_dev(r)).start()
+
+        pass_over(got, t)
+
+        @pl.when(t < 2)
+        def _():
+            ref = h_spot(t, mine)
+            arrived(ref, h_send.at[t], h_recv.at[t])
+            remote(ref, ref, x_send.at[1 - r, t], x_recv.at[1 - r, t], x_dev(1 - r)).start()
+            remote(ref, ref, y_send.at[t + 2], y_recv.at[t + 2], y_far).start()
+            pass_over(ref, 14 + t)
+
+        @pl.when((t > 0) & (t < 11))
+        def _():
+            ref = spot(par, plane(sig * (lax.div(t + 3, 2) - 1)), r)
+            remote(ref, ref, y_send.at[t + 3], y_recv.at[t + 3], y_far).start()
+
+        ref = y_spot(t, mine)
+        arrived(ref, y_send.at[t], y_recv.at[t])
+
+        @pl.when(t < 13)
+        def _():
+            i = jnp.where(t < 2, 13, t)
+            remote(ref, ref, x_send.at[1 - r, i], x_recv.at[1 - r, i], x_dev(1 - r)).start()
+
+        pass_over(ref, 16 + t)
+
+        def pass_near(first, last):
+            @pl.loop(first, jnp.minimum(last, GROUPS))
+            def _(g):
+                for which in range(2):
+                    ref = slot(near, which, g)
+                    arrived(ref, near_send.at[which, g], near_recv.at[which, g])
+                    remote(
+                        ref, slot(far, which, g), far_send.at[which, g], far_recv.at[which, g], h_out
+                    ).start()
+
+        def near_here(half):
+            return lax.div(half * 25, 64)
+
+        pass_near(near_here(2 * t + 1), near_here(2 * t + 2))
+
+        def far_here(s):
+            return lax.div(jnp.maximum((s - 1) * 25 - 8, 0), 32)
+
+        @pl.loop(far_here(t - 1), far_here(t))
         def _(g):
-            for which in range(2):
-                ref = slot(near, which, g)
-                arrived(ref, near_send.at[which, g], near_recv.at[which, g])
-                remote(ref, slot(far, which, g), far_send.at[which, g], far_recv.at[which, g], h_out).start()
-
-        @pl.when(t >= 2)
+            attend_group(g)
+
+        @pl.when(t >= 1)
         def _():
             for r in range(2):
-                ref = x_spot(r, t - 2, 1 - mine)
-                arrived(ref, x_send.at[r, t - 2], x_recv.at[r, t - 2])
-                pass_over(ref, 30 + r * 13 + t - 2)
-
-        @pl.when(t == 3)
+                ref = x_spot(r, t - 1, 1 - mine)
+                arrived(ref, x_send.at[r, t - 1], x_recv.at[r, t - 1])
+                pass_over(ref, 30 + r * 13 + t - 1)
+
+        @pl.when(t == 2)
         def _():
             for r in range(2):
                 ref = piece(1 - par, z, 1 - mine, r)
                 arrived(ref, x_send.at[r, 13], x_recv.at[r, 13])
                 pass_over(ref, 56 + r)
 
-        @pl.when(t == 10)
+        @pl.when(t == 9)
         def _():
             ref = piece(par, plane(5 * sig), 1 - mine, 0)
             remote(ref, ref, d_send.at[0], d_recv.at[0], y_near).start()
 
-        @pl.when(t == 13)
+        @pl.when(t == 12)
         def _():
             ref = piece(par, plane(6 * sig), 1 - mine, 1)
             remote(ref, ref, d_send.at[1], d_recv.at[1], y_near).start()
 
-        def ready(s):
-            return lax.div(jnp.maximum(s - 2, 0) * 25, 32)
-
-        @pl.loop(ready(t), jnp.minimum(ready(t + 1), GROUPS))
-        def _(g):
-            for which in range(2):
-                arrived(slot(far, which, g), far_send.at[which, g], far_recv.at[which, g])
-
-            @pl.loop(0, 2)
-            def _(i):
-                attend(2 * g + i)
+        pass_near(near_here(2 * t + 2), near_here(2 * t + 3))
 
         @pl.when(t >= 1)
         def _():
@@ -297,12 +312,12 @@
         def _():
             handed(14 + t - 1)
 
-        @pl.when(t >= 3)
-        def _():
-            handed(30 + t - 3)
-            handed(43 + t - 3)
-
-        @pl.when(t == 4)
+        @pl.when(t >= 2)
+        def _():
+            handed(30 + t - 2)
+            handed(43 + t - 2)
+
+        @pl.when(t == 3)
         def _():
             handed(56)
             handed(57)
@@ -314,24 +329,12 @@
         arrived(ref, d_send.at[i], d_recv.at[i])
         pass_over(ref, 58 + i)
 
-    for i in (42, 55, 58, 59):
+    attend_group(GROUPS - 1)
+
+    for i in (13, 29, 42, 55, 58, 59):
         handed(i)
 
-    @pl.loop(0, 4)
-    def _(j):
-        @pl.when(jnp.maximum(due(2 * j), due(2 * j + 1)) == LAST)
-        def _():
-            accumulate(640 * j + 256, 128)
-
-    ends = [pl.ds(pl.multiple_of(first_row(plane(m * sig)), HEAD_SIZE), 256) for m in (2, 3)]
-
-    @pl.loop(0, D // COLS)
-    def _(n):
-        cols = pl.ds(pl.multiple_of(n * COLS, COLS), COLS)
-        product = total[:, cols]
-        for rows in ends:
-            product += jnp.dot(ctx[:, rows], weight[rows, cols], preferred_element_type=jnp.float32)
-        out[:, cols] = product.astype(jnp.bfloat16)
+    project(TICKS)
 
     def sent(ref, send, recv):
         remote(ref, ref, send, recv, other).wait_send()
@@ -361,9 +364,9 @@
 def local(query_frames, key_frames, value_frames, stream, out_weight):
     dma = pltpu.SemaphoreType.DMA
     bf16 = jnp.bfloat16
-    return pl.pallas_call(
+    total = pl.pallas_call(
         kernel,
-        out_shape=jax.ShapeDtypeStruct((BLOCK, D), bf16),
+        out_shape=jax.ShapeDtypeStruct((BLOCK, D), jnp.float32),
         in_specs=[pl.BlockSpec(memory_space=pltpu.HBM)] * 5,
         out_specs=pl.BlockSpec(memory_space=pltpu.VMEM),
         scratch_shapes=[
@@ -374,7 +377,6 @@
             pltpu.VMEM((BLOCK, WIDTH), bf16),
             pltpu.VMEM((BLOCK, D), bf16),
             pltpu.VMEM((WIDTH, D), bf16),
-            pltpu.VMEM((BLOCK, D), jnp.float32),
             dma((5,)),
             dma((14,)), dma((14,)),
             dma((2,)), dma((2,)),
@@ -386,9 +388,10 @@
             dma((2, GROUPS)), dma((2, GROUPS)),
         ],
         compiler_params=pltpu.CompilerParams(
-            collective_id=0, has_side_effects=True, vmem_limit_bytes=50 * 1024 * 1024
+            collective_id=0, has_side_effects=True, vmem_limit_bytes=44 * 1024 * 1024
         ),
     )(*[pltpu.with_memory_space_constraint(a, pltpu.HBM) for a in (query_frames, key_frames, value_frames, stream, out_weight)])
+    return total.astype(bf16)
 
 
 def solution(mesh):

time: 97.6 us -> 94.1 us (0.964)
  Pallas kernels: 96 us -> 92.2 us
  other arithmetic: 0 us -> 1.85 us
  local copies, waits for them, and re-layouts: 1.49 us -> 0 us
    pallas_call x1, Pallas kernels: 96 us -> 92.2 us  [local(): pl.pallas_call(kernel, out_shape=jax.ShapeDtypeStruct((BLOCK, D), jnp.flo...]
    convert_element_type x0 -> x1, other arithmetic: none -> 1.85 us  [local(): return total.astype(bf16)]
    unnamed x1 -> x0, local copies, waits for them, and re-layouts: 1.49 us -> none
where the time goes in v3:
time: 94.1 us; the launch traced here: 94 us
  Pallas kernels  92.2 us (98%)
  other arithmetic  1.85 us (2%)
    pallas_call x1, Pallas kernels, local(): pl.pallas_call(kernel, out_shape=jax.ShapeDtypeStruct((BLOCK, D), jnp.flo...  92.2 us

profile of v3, /device:TPU:1, one launch (start us, length us, event | category | flops | bytes accessed | tf_op | source)
XLA Modules:
  0.0 94.0 jit_solution(12822030417993579620)
XLA Ops:
  0.0 92.2 %shard_map.55 = f32[256,5120]{1,0:T(8,128)S(1)} custom-call(bf16[256,2560]{1,0:T(8,128)(2,1)} %q_hbm.1, bf16[256,2560]{1,0:T(8,128)(2,1)} %k_hbm.1, bf16[256,2560]{1,0:T(8,128)(2,1)} %v_hbm.1, bf16[256,5120]{1,0:T(8,128)(2,1)} %stream_hbm.1, bf16[160,5120]{1,0:T(8,128)(2,1)} %w_hbm.1), custom_call_target="tpu_custom_call" | custom-call | tf_op jit(solution)/shard_map/pallas_call | solution.py:367
  92.2 1.9 %convert_element_type.3 = bf16[256,5120]{1,0:T(8,128)(2,1)} convert(f32[256,5120]{1,0:T(8,128)S(1)} %shard_map.55) | non-fusion elementwise | flops 1310720 | bytes 7864320 | tf_op jit(solution)/shard_map/convert_element_type | solution.py:394

commit v4 on v3

--- a/solution.py
+++ b/solution.py
@@ -173,10 +173,7 @@
     def accumulate(row, depth):
         rows = pl.ds(pl.multiple_of(row, HEAD_SIZE), depth)
 
-        @pl.loop(0, D // WIDTH)
-        def _(n):
-            cols = pl.ds(pl.multiple_of(n * WIDTH, WIDTH), WIDTH)
-            total[:, cols] += jnp.dot(ctx[:, rows], weight[rows, cols], preferred_element_type=jnp.float32)
+        total[...] += jnp.dot(ctx[:, rows], weight[rows, :], preferred_element_type=jnp.float32)
 
     def due(zz):
         m = lax.rem(sig * (zz - z) + 16, 8)
@@ -226,7 +223,7 @@
 
         r = lax.rem(t, 2)
 
-        @pl.when(t < 13)
+        @pl.when(t < 12)
         def _():
             remote(got, got, x_send.at[r, t], x_recv.at[r, t], x_dev(r)).start()
 
@@ -238,7 +235,7 @@
             arrived(ref, h_send.at[t], h_recv.at[t])
             remote(ref, ref, x_send.at[1 - r, t], x_recv.at[1 - r, t], x_dev(1 - r)).start()
             remote(ref, ref, y_send.at[t + 2], y_recv.at[t + 2], y_far).start()
-            pass_over(ref, 14 + t)
+            pass_over(ref, 15 + t)
 
         @pl.when((t > 0) & (t < 11))
         def _():
@@ -248,12 +245,40 @@
         ref = y_spot(t, mine)
         arrived(ref, y_send.at[t], y_recv.at[t])
 
-        @pl.when(t < 13)
-        def _():
-            i = jnp.where(t < 2, 13, t)
+        @pl.when(t < 12)
+        def _():
+            i = jnp.where(t < 2, 12, t)
             remote(ref, ref, x_send.at[1 - r, i], x_recv.at[1 - r, i], x_dev(1 - r)).start()
 
-        pass_over(ref, 16 + t)
+        pass_over(ref, 17 + t)
+
+        @pl.when(t >= 2)
+        def _():
+            for side in range(2):
+                ref = x_spot(side, t - 2, 1 - mine)
+                arrived(ref, x_send.at[side, t - 2], x_recv.at[side, t - 2])
+                pass_over(ref, 32 + side * 12 + t - 2)
+
+        @pl.when(t == 3)
+        def _():
+            for side in range(2):
+                ref = piece(1 - par, z, 1 - mine, side)
+                arrived(ref, x_send.at[side, 12], x_recv.at[side, 12])
+                pass_over(ref, 56 + side)
+
+        @pl.when(t == 11)
+        def _():
+            ref = piece(par, plane(5 * sig), 1 - mine, 0)
+            remote(ref, ref, y_send.at[14], y_recv.at[14], y_far).start()
+            ref = piece(par, plane(5 * sig), 1 - mine, 1)
+            remote(ref, ref, d_send.at[0], d_recv.at[0], y_near).start()
+
+        @pl.when(t == 12)
+        def _():
+            ref = piece(1 - par, plane(-7 * sig), 1 - mine, 1)
+            remote(ref, ref, z_send.at[14], z_recv.at[14], z_out).start()
+            ref = piece(par, plane(6 * sig), 1 - mine, 0)
+            remote(ref, ref, d_send.at[1], d_recv.at[1], y_near).start()
 
         def pass_near(first, last):
             @pl.loop(first, jnp.minimum(last, GROUPS))
@@ -277,45 +302,21 @@
         def _(g):
             attend_group(g)
 
+        pass_near(near_here(2 * t + 2), near_here(2 * t + 3))
+
         @pl.when(t >= 1)
         def _():
-            for r in range(2):
-                ref = x_spot(r, t - 1, 1 - mine)
-                arrived(ref, x_send.at[r, t - 1], x_recv.at[r, t - 1])
-                pass_over(ref, 30 + r * 13 + t - 1)
-
-        @pl.when(t == 2)
-        def _():
-            for r in range(2):
-                ref = piece(1 - par, z, 1 - mine, r)
-                arrived(ref, x_send.at[r, 13], x_recv.at[r, 13])
-                pass_over(ref, 56 + r)
-
-        @pl.when(t == 9)
-        def _():
-            ref = piece(par, plane(5 * sig), 1 - mine, 0)
-            remote(ref, ref, d_send.at[0], d_recv.at[0], y_near).start()
-
-        @pl.when(t == 12)
-        def _():
-            ref = piece(par, plane(6 * sig), 1 - mine, 1)
-            remote(ref, ref, d_send.at[1], d_recv.at[1], y_near).start()
-
-        pass_near(near_here(2 * t + 2), near_here(2 * t + 3))
-
-        @pl.when(t >= 1)
-        def _():
             handed(t - 1)
-            handed(16 + t - 1)
+            handed(17 + t - 1)
 
         @pl.when((t == 1) | (t == 2))
         def _():
-            handed(14 + t - 1)
+            handed(15 + t - 1)
 
         @pl.when(t >= 2)
         def _():
-            handed(30 + t - 2)
-            handed(43 + t - 2)
+            handed(32 + t - 2)
+            handed(44 + t - 2)
 
         @pl.when(t == 3)
         def _():
@@ -324,14 +325,18 @@
 
         project(t)
 
-    for i in range(2):
-        ref = piece(1 - par, plane(-(5 + i) * sig), 1 - mine, i)
-        arrived(ref, d_send.at[i], d_recv.at[i])
-        pass_over(ref, 58 + i)
-
+    def last(send, recv, step, r, i):
+        ref = piece(1 - par, plane(-step * sig), 1 - mine, r)
+        arrived(ref, send, recv)
+        pass_over(ref, i)
+
+    last(d_send.at[0], d_recv.at[0], 5, 1, 58)
+    last(d_send.at[1], d_recv.at[1], 6, 0, 59)
+    last(y_send.at[14], y_recv.at[14], 5, 0, 31)
+    last(z_send.at[14], z_recv.at[14], 6, 1, 14)
     attend_group(GROUPS - 1)
 
-    for i in (13, 29, 42, 55, 58, 59):
+    for i in (13, 30, 14, 31, 58, 59):
         handed(i)
 
     project(TICKS)
@@ -339,10 +344,13 @@
     def sent(ref, send, recv):
         remote(ref, ref, send, recv, other).wait_send()
 
-    @pl.loop(0, 14)
+    @pl.loop(0, 15)
     def _(i):
         sent(any_piece, z_send.at[i], z_recv.at[i])
         sent(any_piece, y_send.at[i], y_recv.at[i])
+
+    @pl.loop(0, 13)
+    def _(i):
         for r in range(2):
             sent(any_piece, x_send.at[r, i], x_recv.at[r, i])
 
@@ -378,10 +386,10 @@
             pltpu.VMEM((BLOCK, D), bf16),
             pltpu.VMEM((WIDTH, D), bf16),
             dma((5,)),
-            dma((14,)), dma((14,)),
+            dma((15,)), dma((15,)),
             dma((2,)), dma((2,)),
-            dma((14,)), dma((14,)),
-            dma((2, 14)), dma((2, 14)),
+            dma((15,)), dma((15,)),
+            dma((2, 13)), dma((2, 13)),
             dma((2,)), dma((2,)),
             dma((60,)), dma((60,)),
             dma((2, GROUPS)), dma((2, GROUPS)),

time: 94.1 us -> 90.5 us (0.962)
  Pallas kernels: 92.2 us -> 88.6 us
    pallas_call x1, Pallas kernels: 92.2 us -> 88.6 us  [local(): pl.pallas_call(kernel, out_shape=jax.ShapeDtypeStruct((BLOCK, D), jnp.flo...]
where the time goes in v4:
time: 90.5 us; the launch traced here: 90.4 us
  Pallas kernels  88.6 us (98%)
  other arithmetic  1.85 us (2%)
    pallas_call x1, Pallas kernels, local(): pl.pallas_call(kernel, out_shape=jax.ShapeDtypeStruct((BLOCK, D), jnp.flo...  88.6 us
    convert_element_type x1, other arithmetic, local(): return total.astype(bf16)  1.85 us

profile of v4, /device:TPU:1, one launch (start us, length us, event | category | flops | bytes accessed | tf_op | source)
XLA Modules:
  0.0 90.4 jit_solution(7010654182991242991)
XLA Ops:
  0.0 88.6 %shard_map.55 = f32[256,5120]{1,0:T(8,128)S(1)} custom-call(bf16[256,2560]{1,0:T(8,128)(2,1)} %q_hbm.1, bf16[256,2560]{1,0:T(8,128)(2,1)} %k_hbm.1, bf16[256,2560]{1,0:T(8,128)(2,1)} %v_hbm.1, bf16[256,5120]{1,0:T(8,128)(2,1)} %stream_hbm.1, bf16[160,5120]{1,0:T(8,128)(2,1)} %w_hbm.1), custom_call_target="tpu_custom_call" | custom-call | tf_op jit(solution)/shard_map/pallas_call | solution.py:375
  88.6 1.9 %convert_element_type.3 = bf16[256,5120]{1,0:T(8,128)(2,1)} convert(f32[256,5120]{1,0:T(8,128)S(1)} %shard_map.55) | non-fusion elementwise | flops 1310720 | bytes 7864320 | tf_op jit(solution)/shard_map/convert_element_type | solution.py:402

commit v5 on v4

--- a/solution.py
+++ b/solution.py
@@ -252,34 +252,6 @@
 
         pass_over(ref, 17 + t)
 
-        @pl.when(t >= 2)
-        def _():
-            for side in range(2):
-                ref = x_spot(side, t - 2, 1 - mine)
-                arrived(ref, x_send.at[side, t - 2], x_recv.at[side, t - 2])
-                pass_over(ref, 32 + side * 12 + t - 2)
-
-        @pl.when(t == 3)
-        def _():
-            for side in range(2):
-                ref = piece(1 - par, z, 1 - mine, side)
-                arrived(ref, x_send.at[side, 12], x_recv.at[side, 12])
-                pass_over(ref, 56 + side)
-
-        @pl.when(t == 11)
-        def _():
-            ref = piece(par, plane(5 * sig), 1 - mine, 0)
-            remote(ref, ref, y_send.at[14], y_recv.at[14], y_far).start()
-            ref = piece(par, plane(5 * sig), 1 - mine, 1)
-            remote(ref, ref, d_send.at[0], d_recv.at[0], y_near).start()
-
-        @pl.when(t == 12)
-        def _():
-            ref = piece(1 - par, plane(-7 * sig), 1 - mine, 1)
-            remote(ref, ref, z_send.at[14], z_recv.at[14], z_out).start()
-            ref = piece(par, plane(6 * sig), 1 - mine, 0)
-            remote(ref, ref, d_send.at[1], d_recv.at[1], y_near).start()
-
         def pass_near(first, last):
             @pl.loop(first, jnp.minimum(last, GROUPS))
             def _(g):
@@ -301,6 +273,34 @@
         @pl.loop(far_here(t - 1), far_here(t))
         def _(g):
             attend_group(g)
+
+        @pl.when(t >= 2)
+        def _():
+            for side in range(2):
+                ref = x_spot(side, t - 2, 1 - mine)
+                arrived(ref, x_send.at[side, t - 2], x_recv.at[side, t - 2])
+                pass_over(ref, 32 + side * 12 + t - 2)
+
+        @pl.when(t == 3)
+        def _():
+            for side in range(2):
+                ref = piece(1 - par, z, 1 - mine, side)
+                arrived(ref, x_send.at[side, 12], x_recv.at[side, 12])
+                pass_over(ref, 56 + side)
+
+        @pl.when(t == 11)
+        def _():
+            ref = piece(par, plane(5 * sig), 1 - mine, 0)
+            remote(ref, ref, y_send.at[14], y_recv.at[14], y_far).start()
+            ref = piece(par, plane(5 * sig), 1 - mine, 1)
+            remote(ref, ref, d_send.at[0], d_recv.at[0], y_near).start()
+
+        @pl.when(t == 12)
+        def _():
+            ref = piece(1 - par, plane(-7 * sig), 1 - mine, 1)
+            remote(ref, ref, z_send.at[14], z_recv.at[14], z_out).start()
+            ref = piece(par, plane(6 * sig), 1 - mine, 0)
+            remote(ref, ref, d_send.at[1], d_recv.at[1], y_near).start()
 
         pass_near(near_here(2 * t + 2), near_here(2 * t + 3))
 

time: 90.5 us -> 91.5 us (1.011)
  Pallas kernels: 88.6 us -> 89.6 us
    pallas_call x1, Pallas kernels: 88.6 us -> 89.6 us  [local(): pl.pallas_call(kernel, out_shape=jax.ShapeDtypeStruct((BLOCK, D), jnp.flo...]
where the time goes in v5:
time: 91.5 us; the launch traced here: 91.4 us
  Pallas kernels  89.6 us (98%)
  other arithmetic  1.85 us (2%)
    pallas_call x1, Pallas kernels, local(): pl.pallas_call(kernel, out_shape=jax.ShapeDtypeStruct((BLOCK, D), jnp.flo...  89.6 us
    convert_element_type x1, other arithmetic, local(): return total.astype(bf16)  1.85 us

profile of v5, /device:TPU:1, one launch (start us, length us, event | category | flops | bytes accessed | tf_op | source)
XLA Modules:
  0.0 91.4 jit_solution(9061239255340757906)
XLA Ops:
  0.0 89.6 %shard_map.55 = f32[256,5120]{1,0:T(8,128)S(1)} custom-call(bf16[256,2560]{1,0:T(8,128)(2,1)} %q_hbm.1, bf16[256,2560]{1,0:T(8,128)(2,1)} %k_hbm.1, bf16[256,2560]{1,0:T(8,128)(2,1)} %v_hbm.1, bf16[256,5120]{1,0:T(8,128)(2,1)} %stream_hbm.1, bf16[160,5120]{1,0:T(8,128)(2,1)} %w_hbm.1), custom_call_target="tpu_custom_call" | custom-call | tf_op jit(solution)/shard_map/pallas_call | solution.py:375
  89.6 1.9 %convert_element_type.3 = bf16[256,5120]{1,0:T(8,128)(2,1)} convert(f32[256,5120]{1,0:T(8,128)S(1)} %shard_map.55) | non-fusion elementwise | flops 1310720 | bytes 7864320 | tf_op jit(solution)/shard_map/convert_element_type | solution.py:402
